TPU v7x, 256 devices: a whole 4x4x8 slice. The times are simulated.
256 devices in a mesh: row: 8 (over z), col: 16 (over y, x), pan: 2 (over core).
Axes of the slice: x: 4, y: 4, z: 8, core: 2. Of those that a mesh axis runs over, the one named last changes fastest.
Arguments:
- plan_values: bfloat16 [8192, 128, 256], P('row', 'col', 'pan'), may hold values from 0.099609375 to 1
- plan_blocks: int32 [8, 128], P('row', 'col'), may hold values from 0 to 127, as said below
- first_values: bfloat16 [32, 3, 256, 256], P('row'), may hold values from -0.21875 to 0.21875
- first_blocks: int32 [32, 3], P('row'), may hold values from 0 to 3, as said below
- second_values: bfloat16 [128, 6, 256, 256], P('col', None, None, 'pan'), may hold values from -0.15625 to 0.15625
- second_blocks: int32 [128, 6], P('col'), may hold values from 0 to 7, as said below
- weight_first: float32 [8192], P('row'), may hold values from 0.5 to 2
- weight_second: float32 [128, 256], P('col', 'pan'), may hold values from 0.5 to 2
- offset_first: float32 [8192], P('row'), may hold values from -3 to 3
- offset_second: float32 [128, 256], P('col', 'pan'), may hold values from -3 to 3
Outputs:
- new_plan: bfloat16 [8192, 128, 256], P('row', 'col', 'pan')
- scale_first: float32 [8192], P('row')
- scale_second: float32 [128, 256], P('col', 'pan')
Inputs may be any that keep to these rules, and one draw needn't show every extreme that they name: `plan_blocks`: each entry is a slice-B block number; its column panel is the entry // 8. Within the 8 slots of one index of col (aligned groups of the second dimension) no column panel is named more than 2 times, and in every row panel one column panel is named exactly 2 times by every such group. `first_blocks`: block numbers within the row panel of the slice-A block; the 3 entries of a row are distinct. `second_blocks`: block numbers within the column panel of the slice-B block; the 6 entries of a row are distinct.
All inputs are finite; a program needn't handle non-finite values.
Results may differ from a plain program's by a relative error of at most 0.0087.
Values may be sent and summed in bfloat16 or wider, within the bound.
No kernel may reach another device: no remote copies, remote signals or barrier semaphores. Data moves between devices by JAX's collectives and lax.ppermute only.
A program may use at most 128 MiB of HBM per device.

v0:
```python
import jax
import jax.numpy as jnp
from jax import lax
from jax.sharding import PartitionSpec as P

CAP = 2


def first_product(plan_values, first_values, first_blocks):
    tile_count = first_blocks.shape[0]
    block_size = first_values.shape[2]
    slot_count = plan_values.shape[1]
    half_width = plan_values.shape[2]
    row_tiles = plan_values.reshape(tile_count, block_size, slot_count * half_width)
    running = jnp.zeros(row_tiles.shape, jnp.float32)
    for neighbor in range(first_blocks.shape[1]):
        picked = jnp.take(row_tiles, first_blocks[:, neighbor], axis=0)
        running = running + jnp.einsum(
            "iab,ibn->ian", first_values[:, neighbor], picked, preferred_element_type=jnp.float32
        )
    return running.astype(jnp.bfloat16).reshape(tile_count * block_size, slot_count, half_width)


def dispatch(chooser, within_panel, product):
    outgoing = jnp.einsum(
        "dcs,rsh->dcrh", chooser.astype(jnp.bfloat16), product, preferred_element_type=jnp.float32
    ).astype(jnp.bfloat16)
    labels = jnp.sum(chooser.astype(jnp.int32) * (within_panel + 1)[None, None, :], axis=2) - 1
    return (outgoing, labels)


def second_product(dense_plan, second_values, second_blocks):
    blocks_here = second_blocks.shape[0]
    columns = jnp.arange(blocks_here)
    placer = (second_blocks[:, :, None] == columns[None, None, :]).astype(jnp.bfloat16)
    panel_matrix = jnp.einsum(
        "kqbh,kql->kblh", second_values, placer, preferred_element_type=jnp.float32
    ).astype(jnp.bfloat16)
    return jnp.einsum("rkb,kblh->rlh", dense_plan, panel_matrix, preferred_element_type=jnp.float32)


def local(
    plan_values,
    plan_blocks,
    first_values,
    first_blocks,
    second_values,
    second_blocks,
    weight_first,
    weight_second,
    offset_first,
    offset_second,
):
    col_count = lax.axis_size("col")
    blocks_here = second_blocks.shape[0]
    slot_count = plan_values.shape[1]
    block_size = first_values.shape[2]
    panel_rows = plan_values.shape[0]
    plan_width = float(slot_count * col_count * block_size)
    named_blocks = plan_blocks[0]
    target_panel = named_blocks // blocks_here
    within_panel = named_blocks % blocks_here
    same_panel = target_panel[:, None] == target_panel[None, :]
    earlier = jnp.arange(slot_count)[:, None] > jnp.arange(slot_count)[None, :]
    position = jnp.sum((same_panel & earlier).astype(jnp.int32), axis=1)
    chooser = (target_panel[None, None, :] == jnp.arange(col_count)[:, None, None]) & (
        position[None, None, :] == jnp.arange(CAP)[None, :, None]
    )
    product = first_product(plan_values, first_values, first_blocks)
    outgoing, labels = dispatch(chooser, within_panel, product)
    incoming, arrival_ids = (
        lax.all_to_all(outgoing, "col", split_axis=0, concat_axis=0, tiled=True),
        lax.all_to_all(labels, "col", split_axis=0, concat_axis=0, tiled=True),
    )
    item_rows = incoming.shape[2]
    arrivals = incoming.reshape(col_count * CAP, item_rows, incoming.shape[3])
    matcher = (arrival_ids.reshape(-1)[:, None] == jnp.arange(blocks_here)[None, :]).astype(
        jnp.bfloat16
    )
    dense_plan = jnp.einsum(
        "ik,irh->rkh", matcher, arrivals, preferred_element_type=jnp.float32
    ).astype(jnp.bfloat16)
    present = jnp.minimum(jnp.sum(matcher.astype(jnp.float32), axis=0), 1.0)
    gathered = lax.all_gather(dense_plan, "pan", axis=2, tiled=True)
    crossed = second_product(gathered, second_values, second_blocks)
    kernel_values = present[None, :, None] * jnp.exp(
        crossed - offset_first[:, None, None] - offset_second[None]
    )
    row_totals = lax.psum(jnp.sum(kernel_values, axis=(1, 2)), ("col", "pan"))
    scale_first = weight_first * plan_width / row_totals
    weighted = kernel_values * scale_first[:, None, None]
    colsum, counts = lax.psum((jnp.sum(weighted, axis=0), present * float(panel_rows)), "row")
    scale_second = weight_second * counts[:, None] / jnp.where(counts[:, None] > 0, colsum, 1.0)
    new_values = (weighted * scale_second[None]).astype(jnp.bfloat16)
    returned = jnp.einsum(
        "ik,rkh->irh", matcher, new_values, preferred_element_type=jnp.float32
    ).astype(jnp.bfloat16)
    returned = returned.reshape(col_count, CAP, item_rows, returned.shape[2])
    homeward = lax.all_to_all(returned, "col", split_axis=0, concat_axis=0, tiled=True)
    new_plan = jnp.einsum(
        "dcs,dcrh->rsh", chooser.astype(jnp.bfloat16), homeward, preferred_element_type=jnp.float32
    ).astype(jnp.bfloat16)
    return (new_plan, scale_first, scale_second)


def solution(mesh):
    return jax.shard_map(
        local,
        mesh=mesh,
        in_specs=(
            P("row", "col", "pan"),
            P("row", "col"),
            P("row", None, None, None),
            P("row", None),
            P("col", None, None, "pan"),
            P("col", None),
            P("row"),
            P("col", "pan"),
            P("row"),
            P("col", "pan"),
        ),
        out_specs=(P("row", "col", "pan"), P("row"), P("col", "pan")),
        check_vma=False,
    )
```

profile of v0, /device:TPU:2, one launch (start us, length us, event | category | flops | bytes accessed | tf_op | source)
XLA Modules:
  0.0 442.7 jit_solution(4532502949180978923)
XLA Ops:
  9.8 7.5 %all-to-all-start = ((s32[16,1,2]{2,1,0:T(1,128)}), s32[16,1,2]{2,1,0:T(1,128)S(1)}, u32[]{:S(2)}, u32[]{:S(2)}) async-start(s32[16,1,2]{2,1,0:T(1,128)} %copy.46), calls=%async_computation | async-start | bytes 16384 | tf_op jit(solution)/shard_map/all_to_all | solution.py:73
  18.4 4.2 reshape.172
  22.6 3.6 gather_fusion.1
  26.1 3.6 gather_fusion.2
  29.7 3.6 gather_fusion
  33.3 2.8 fusion.20
  37.8 2.7 fusion.29
  40.5 4.0 copy.53
  46.7 5.1 %convolution_convert_fusion.1 = bf16[16,2,1024,128]{3,0,2,1:T(8,128)(2,1)} fusion(bf16[1024,8,128,1]{2,1,0,3:T(8,128)(2,1)S(1)} %bitcast.93, pred[2,8]{1,0:T(4,128)(4,1)S(1)} %iota_compare_fusion.4, pred[16,8]{0,1:T(8,128)(4,1)S(1)} %iota_compare_fusion.3), kind=kOutput, calls=%fused_computation.8 | convolution fusion | flops 71303424 | bytes 10485904 | tf_op jit(solution)/shard_map/dcs,rsh->dcrh/dot_general | solution.py:25
  51.8 8.8 %copy.54 = bf16[16,2,1024,128]{3,2,1,0:T(8,128)(2,1)} copy(bf16[16,2,1024,128]{3,0,2,1:T(8,128)(2,1)} %convolution_convert_fusion.1) | data formatting | bytes 16777216 | tf_op jit(solution)/shard_map/convert_element_type | solution.py:27
  60.6 7.2 %all-to-all-start.1 = ((bf16[16,2,1024,128]{3,2,1,0:T(8,128)(2,1)}), bf16[16,2,1024,128]{3,2,1,0:T(8,128)(2,1)}, u32[]{:S(2)}, u32[]{:S(2)}) async-start(bf16[16,2,1024,128]{3,2,1,0:T(8,128)(2,1)} %copy.54), calls=%async_computation.1 | async-start | bytes 16777216 | tf_op jit(solution)/shard_map/all_to_all | solution.py:72
  69.3 118.5 %all-to-all-done.1 = bf16[16,2,1024,128]{3,2,1,0:T(8,128)(2,1)} async-done(((bf16[16,2,1024,128]{3,2,1,0:T(8,128)(2,1)}), bf16[16,2,1024,128]{3,2,1,0:T(8,128)(2,1)}, u32[]{:S(2)}, u32[]{:S(2)}) %all-to-all-start.1) | async-done | bytes 8388640 | tf_op jit(solution)/shard_map/all_to_all | solution.py:72
  187.9 9.3 %convert_bitcast_fusion.1 = bf16[1024,8,128]{2,1,0:T(8,128)(2,1)} fusion(bf16[32,1024,128]{2,1,0:T(8,128)(2,1)} %bitcast.10, s32[32]{0:T(128)S(1)} %eq.91), kind=kOutput, calls=%fused_computation.31 | convolution fusion | flops 68157696 | bytes 10485888 | tf_op jit(solution)/shard_map/ik,irh->rkh/dot_general | solution.py:80
  197.3 4.0 convert_bitcast_fusion
  201.3 18.2 %all-gather.2.cloned.1.call-done = bf16[1024,8,256]{2,1,0:T(8,128)(2,1)} async-done(((bf16[1024,8,128]{2,1,0:T(8,128)(2,1)}), bf16[1024,8,256]{2,1,0:T(8,128)(2,1)}) %all-gather.2.cloned.1.call-update) | async-done | bytes 4194320 | tf_op jit(solution)/shard_map/all_gather | solution.py:84
  219.5 10.1 %fusion.15 = (f32[1024]{0:T(1024)S(1)}, f32[1024,8,128,1]{2,0,3,1:T(8,128)}) fusion(f32[8,128]{1,0:T(8,128)S(1)} %copy-done.7, f32[1024]{0:T(1024)S(1)} %copy-done.8, f32[8]{0:T(128)S(1)} %get-tuple-element.10, bf16[8,256,8,128]{3,2,1,0:T(8,128)(2,1)} %convert_bitcast_fusion, bf16[1024,8,256]{2,1,0:T(8,128)(2,1)} %all-gather.2.cloned.1.call-done), kind=kOutput, calls=%fused_computation.24 | convolution fusion | flops 4299160576 | bytes 12595232 | tf_op jit(solution)/shard_map/rkb,kblh->rlh/dot_general | solution.py:39
  229.6 62.6 %psum.21 = f32[1024]{0:T(1024)S(1)} all-reduce(f32[1024]{0:T(1024)S(1)} %get-tuple-element.13), channel_id=1, replica_groups=mesh['row'=8,'col'=16,'pan'=2] {'col','pan'}, use_global_device_ids=true, to_apply=%region_4.6 | all-reduce | flops 1024 | bytes 8192 | tf_op jit(solution)/shard_map/psum | solution.py:89
  292.2 3.3 multiply_reduce_fusion
  295.5 17.7 %all-reduce = (f32[8,128]{1,0:T(8,128)S(1)}, f32[8]{0:T(128)S(1)}) all-reduce(f32[8,128]{1,0:T(8,128)S(1)} %multiply_reduce_fusion, f32[8]{0:T(128)S(1)} %get-tuple-element.9), channel_id=1, replica_groups=mesh['row'=8,'col'=16,'pan'=2] {'row'}, use_global_device_ids=true, to_apply=%region_7.9 | all-reduce | flops 1032 | bytes 8256 | tf_op jit(solution)/shard_map/psum | solution.py:92
  313.3 3.8 multiply_convert_fusion
  317.2 6.3 %convolution_convert_fusion = bf16[32,1024,128]{2,0,1:T(8,128)(2,1)S(1)} fusion(bf16[1024,8,128]{2,0,1:T(8,128)(2,1)S(1)} %multiply_convert_fusion, s32[32]{0:T(128)S(1)} %eq.91), kind=kOutput, calls=%fused_computation.7 | convolution fusion | flops 71303424 | bytes 10485888 | tf_op jit(solution)/shard_map/ik,rkh->irh/dot_general | solution.py:95
  323.5 8.0 %copy.60 = bf16[16,2,1024,128]{3,1,2,0:T(2,128)(2,1)S(1)} copy(bf16[16,2,1024,128]{3,1,0,2:T(2,128)(2,1)S(1)} %bitcast.91) | data formatting | bytes 16777216 | tf_op jit(solution)/shard_map/reshape | solution.py:98
  331.5 98.3 %all_to_all.16 = bf16[16,2,1024,128]{3,1,2,0:T(2,128)(2,1)S(1)} all-to-all(bf16[16,2,1024,128]{3,1,2,0:T(2,128)(2,1)S(1)} %copy.60), channel_id=1, replica_groups=mesh['row'=8,'col'=16,'pan'=2] {'col'}, dimensions={0} | all-to-all | bytes 16777216 | tf_op jit(solution)/shard_map/all_to_all | solution.py:99
  429.9 6.0 %fusion.32 = bf16[1024,8,128]{2,1,0:T(8,128)(2,1)} fusion(bf16[16,2,1024,128]{3,1,2,0:T(2,128)(2,1)S(1)} %all_to_all.16, pred[2,8]{1,0:T(4,128)(4,1)S(1)} %iota_compare_fusion.4, pred[16,8]{0,1:T(8,128)(4,1)S(1)} %iota_compare_fusion.3), kind=kOutput, calls=%fused_computation.36 | convolution fusion | flops 68157696 | bytes 10485904 | tf_op jit(solution)/shard_map/dcs,dcrh->rsh/dot_general | solution.py:100
  (53 shorter events, 9.3 us)
Async XLA Ops:
  7.2 190.1 %copy-start = (bf16[8,6,256,128]{3,2,1,0:T(8,128)(2,1)S(1)}, bf16[8,6,256,128]{3,2,1,0:T(8,128)(2,1)}, u32[]{:S(2)}) copy-start(bf16[8,6,256,128]{3,2,1,0:T(8,128)(2,1)} %param.16) | copy-start | bytes 9437188
  9.8 50.8 %all-to-all-start = ((s32[16,1,2]{2,1,0:T(1,128)}), s32[16,1,2]{2,1,0:T(1,128)S(1)}, u32[]{:S(2)}, u32[]{:S(2)}) async-start(s32[16,1,2]{2,1,0:T(1,128)} %copy.46), calls=%async_computation | async-start | bytes 16384 | tf_op jit(solution)/shard_map/all_to_all | solution.py:73
  33.3 2.8 copy-start.3
  33.3 2.8 copy-start.4
  36.2 1.6 copy-start.2
  60.6 127.3 %all-to-all-start.1 = ((bf16[16,2,1024,128]{3,2,1,0:T(8,128)(2,1)}), bf16[16,2,1024,128]{3,2,1,0:T(8,128)(2,1)}, u32[]{:S(2)}, u32[]{:S(2)}) async-start(bf16[16,2,1024,128]{3,2,1,0:T(8,128)(2,1)} %copy.54), calls=%async_computation.1 | async-start | bytes 16777216 | tf_op jit(solution)/shard_map/all_to_all | solution.py:72
  67.8 151.7 %all-gather.2.cloned.1.call-start = ((), (), s32[]{:S(2)}) async-start(), calls=%async_computation.3 | async-start | bytes 6291456 | tf_op jit(solution)/shard_map/all_gather | solution.py:84
  187.9 9.4 %copy-start.9 = (s32[8,6]{1,0:T(8,128)S(1)}, s32[8,6]{1,0:T(8,128)}, u32[]{:S(2)}) copy-start(s32[8,6]{1,0:T(8,128)} %param.17) | copy-start | bytes 580
  197.2 22.3 %copy-start.7 = (f32[8,128]{1,0:T(8,128)S(1)}, f32[8,128]{1,0:T(8,128)}, u32[]{:S(2)}) copy-start(f32[8,128]{1,0:T(8,128)} %param.21) | copy-start | bytes 12292
  197.3 22.3 %copy-start.8 = (f32[1024]{0:T(1024)S(1)}, f32[1024]{0:T(1024)}, u32[]{:S(2)}) copy-start(f32[1024]{0:T(1024)} %param.20) | copy-start | bytes 12292
  219.5 72.7 %copy-start.10 = (f32[1024]{0:T(1024)S(1)}, f32[1024]{0:T(1024)}, u32[]{:S(2)}) copy-start(f32[1024]{0:T(1024)} %param.18) | copy-start | bytes 12292
  229.6 83.6 %copy-start.11 = (f32[8,128]{1,0:T(8,128)S(1)}, f32[8,128]{1,0:T(8,128)}, u32[]{:S(2)}) copy-start(f32[8,128]{1,0:T(8,128)} %param.19) | copy-start | bytes 12292
  292.2 24.9 %copy-start.5 = (f32[1024]{0:T(1024)}, f32[1024]{0:T(1024)S(1)}, u32[]{:S(2)}) copy-start(f32[1024]{0:T(1024)S(1)} %multiply_divide_fusion) | copy-start | bytes 12292
  313.3 10.2 %copy-start.6 = (f32[8,128]{1,0:T(8,128)}, f32[8,128]{1,0:T(8,128)S(1)}, u32[]{:S(2)}) copy-start(f32[8,128]{1,0:T(8,128)S(1)} %select_divide_fusion) | copy-start | bytes 12292
  331.5 104.3 %copy-start.1 = (bf16[8,6,256,128]{3,2,1,0:T(8,128)(2,1)S(1)}, bf16[8,6,256,128]{3,2,1,0:T(8,128)(2,1)}, u32[]{:S(2)}) copy-start(bf16[8,6,256,128]{3,2,1,0:T(8,128)(2,1)} %param.16) | copy-start | bytes 9437188
Sparse Core Ops, SparseCore 0:
  197.3 22.1 all-gather.1
where the time goes:
time: 443 us
  blocking collectives  179 us (40%)
  waiting for transfers between devices  137 us (31%)
  matrix products  47.4 us (11%)
  local copies, waits for them, and re-layouts  40.8 us (9%)
  starting transfers between devices  14.9 us (3%)
  between operations  14.3 us (3%)
  other arithmetic  10 us (2%)
    all_to_all x1, waiting for transfers between devices, local(): lax.all_to_all(outgoing, 'col', split_axis=0, concat_axis=0, tiled=True)  119 us
    all_to_all x1, blocking collectives, local(): lax.all_to_all(returned, 'col', split_axis=0, concat_axis=0, tiled=True)  98.3 us
    psum x1, blocking collectives, local(): row_totals = lax.psum(jnp.sum(kernel_values, axis=(1, 2)), ('col', 'pan'))  62.6 us
    all_gather x1, waiting for transfers between devices, local(): gathered = lax.all_gather(dense_plan, 'pan', axis=2, tiled=True)  18.2 us
    psum x1, blocking collectives, local(): lax.psum((jnp.sum(weighted, axis=0), present * float(panel_rows)), 'row')  17.7 us
    gather x3, local copies, waits for them, and re-layouts, first_product(): picked = jnp.take(row_tiles, first_blocks[:, neighbor], axis=0)  10.8 us
    dot_general x1, matrix products, second_product(): jnp.einsum('rkb,kblh->rlh', dense_plan, panel_matrix, preferred_element_t...  10.1 us
    dot_general x1, matrix products, local(): jnp.einsum('ik,irh->rkh', matcher, arrivals, preferred_element_type=jnp.f...  9.33 us
  transfers between devices with their start and end apart: 3, of which 2 were waited for; matrix products, arithmetic and copies ran while one was open for 11% of the time, Pallas kernels for 0%

commit v1 on v0

--- a/solution.py
+++ b/solution.py
@@ -86,7 +86,7 @@
     kernel_values = present[None, :, None] * jnp.exp(
         crossed - offset_first[:, None, None] - offset_second[None]
     )
-    row_totals = lax.psum(jnp.sum(kernel_values, axis=(1, 2)), ("col", "pan"))
+    row_totals = lax.psum(lax.psum(jnp.sum(kernel_values, axis=(1, 2)), "col"), "pan")
     scale_first = weight_first * plan_width / row_totals
     weighted = kernel_values * scale_first[:, None, None]
     colsum, counts = lax.psum((jnp.sum(weighted, axis=0), present * float(panel_rows)), "row")

time: 443 us -> 420 us (0.948)
  blocking collectives: 179 us -> 156 us
    psum x1 -> x2, blocking collectives: 62.6 us -> 38.8 us  [the longest x1 36.4 us: local(): lax.psum(jnp.sum(kernel_values, axis=(1, 2)), 'col')]
where the time goes in v1:
time: 420 us
  blocking collectives  156 us (37%)
  waiting for transfers between devices  137 us (33%)
  matrix products  47.4 us (11%)
  local copies, waits for them, and re-layouts  40.8 us (10%)
  starting transfers between devices  14.9 us (4%)
  between operations  14.3 us (3%)
  other arithmetic  10 us (2%)
    all_to_all x1, waiting for transfers between devices, local(): lax.all_to_all(outgoing, 'col', split_axis=0, concat_axis=0, tiled=True)  119 us
    all_to_all x1, blocking collectives, local(): lax.all_to_all(returned, 'col', split_axis=0, concat_axis=0, tiled=True)  99 us
    psum x1, blocking collectives, local(): lax.psum(jnp.sum(kernel_values, axis=(1, 2)), 'col')  36.4 us
    all_gather x1, waiting for transfers between devices, local(): gathered = lax.all_gather(dense_plan, 'pan', axis=2, tiled=True)  18.2 us
    psum x1, blocking collectives, local(): lax.psum((jnp.sum(weighted, axis=0), present * float(panel_rows)), 'row')  17.7 us
    gather x3, local copies, waits for them, and re-layouts, first_product(): picked = jnp.take(row_tiles, first_blocks[:, neighbor], axis=0)  10.8 us
    dot_general x1, matrix products, second_product(): jnp.einsum('rkb,kblh->rlh', dense_plan, panel_matrix, preferred_element_t...  10.1 us
    dot_general x1, matrix products, local(): jnp.einsum('ik,irh->rkh', matcher, arrivals, preferred_element_type=jnp.f...  9.33 us
  transfers between devices with their start and end apart: 3, of which 2 were waited for; matrix products, arithmetic and copies ran while one was open for 11% of the time, Pallas kernels for 0%

profile of v1, /device:TPU:2, one launch (start us, length us, event | category | flops | bytes accessed | tf_op | source)
XLA Modules:
  0.0 419.6 jit_solution(8439263346156953798)
XLA Ops:
  9.8 7.5 %all-to-all-start = ((s32[16,1,2]{2,1,0:T(1,128)}), s32[16,1,2]{2,1,0:T(1,128)S(1)}, u32[]{:S(2)}, u32[]{:S(2)}) async-start(s32[16,1,2]{2,1,0:T(1,128)} %copy.46), calls=%async_computation | async-start | bytes 16384 | tf_op jit(solution)/shard_map/all_to_all | solution.py:73
  18.4 4.2 reshape.172
  22.6 3.6 gather_fusion.1
  26.1 3.6 gather_fusion.2
  29.7 3.6 gather_fusion
  33.3 2.8 fusion.20
  37.8 2.7 fusion.29
  40.5 4.0 copy.53
  46.7 5.1 %convolution_convert_fusion.1 = bf16[16,2,1024,128]{3,0,2,1:T(8,128)(2,1)} fusion(bf16[1024,8,128,1]{2,1,0,3:T(8,128)(2,1)S(1)} %bitcast.93, pred[2,8]{1,0:T(4,128)(4,1)S(1)} %iota_compare_fusion.4, pred[16,8]{0,1:T(8,128)(4,1)S(1)} %iota_compare_fusion.3), kind=kOutput, calls=%fused_computation.8 | convolution fusion | flops 71303424 | bytes 10485904 | tf_op jit(solution)/shard_map/dcs,rsh->dcrh/dot_general | solution.py:25
  51.8 8.8 %copy.54 = bf16[16,2,1024,128]{3,2,1,0:T(8,128)(2,1)} copy(bf16[16,2,1024,128]{3,0,2,1:T(8,128)(2,1)} %convolution_convert_fusion.1) | data formatting | bytes 16777216 | tf_op jit(solution)/shard_map/convert_element_type | solution.py:27
  60.6 7.2 %all-to-all-start.1 = ((bf16[16,2,1024,128]{3,2,1,0:T(8,128)(2,1)}), bf16[16,2,1024,128]{3,2,1,0:T(8,128)(2,1)}, u32[]{:S(2)}, u32[]{:S(2)}) async-start(bf16[16,2,1024,128]{3,2,1,0:T(8,128)(2,1)} %copy.54), calls=%async_computation.1 | async-start | bytes 16777216 | tf_op jit(solution)/shard_map/all_to_all | solution.py:72
  69.3 118.5 %all-to-all-done.1 = bf16[16,2,1024,128]{3,2,1,0:T(8,128)(2,1)} async-done(((bf16[16,2,1024,128]{3,2,1,0:T(8,128)(2,1)}), bf16[16,2,1024,128]{3,2,1,0:T(8,128)(2,1)}, u32[]{:S(2)}, u32[]{:S(2)}) %all-to-all-start.1) | async-done | bytes 8388640 | tf_op jit(solution)/shard_map/all_to_all | solution.py:72
  187.9 9.3 %convert_bitcast_fusion.1 = bf16[1024,8,128]{2,1,0:T(8,128)(2,1)} fusion(bf16[32,1024,128]{2,1,0:T(8,128)(2,1)} %bitcast.10, s32[32]{0:T(128)S(1)} %eq.91), kind=kOutput, calls=%fused_computation.31 | convolution fusion | flops 68157696 | bytes 10485888 | tf_op jit(solution)/shard_map/ik,irh->rkh/dot_general | solution.py:80
  197.3 4.0 convert_bitcast_fusion
  201.3 18.2 %all-gather.2.cloned.1.call-done = bf16[1024,8,256]{2,1,0:T(8,128)(2,1)} async-done(((bf16[1024,8,128]{2,1,0:T(8,128)(2,1)}), bf16[1024,8,256]{2,1,0:T(8,128)(2,1)}) %all-gather.2.cloned.1.call-update) | async-done | bytes 4194320 | tf_op jit(solution)/shard_map/all_gather | solution.py:84
  219.5 10.1 %fusion.15 = (f32[1024]{0:T(1024)S(1)}, f32[1024,8,128,1]{2,0,3,1:T(8,128)}) fusion(f32[8,128]{1,0:T(8,128)S(1)} %copy-done.7, f32[1024]{0:T(1024)S(1)} %copy-done.8, f32[8]{0:T(128)S(1)} %get-tuple-element.10, bf16[8,256,8,128]{3,2,1,0:T(8,128)(2,1)} %convert_bitcast_fusion, bf16[1024,8,256]{2,1,0:T(8,128)(2,1)} %all-gather.2.cloned.1.call-done), kind=kOutput, calls=%fused_computation.24 | convolution fusion | flops 4299160576 | bytes 12595232 | tf_op jit(solution)/shard_map/rkb,kblh->rlh/dot_general | solution.py:39
  229.6 36.4 %psum.28 = f32[1024]{0:T(1024)S(1)} all-reduce(f32[1024]{0:T(1024)S(1)} %get-tuple-element.13), channel_id=1, replica_groups=mesh['row'=8,'col'=16,'pan'=2] {'col'}, use_global_device_ids=true, to_apply=%region_4.6 | all-reduce | flops 1024 | bytes 8192 | tf_op jit(solution)/shard_map/psum | solution.py:89
  268.5 3.3 multiply_reduce_fusion
  271.7 17.7 %all-reduce = (f32[8,128]{1,0:T(8,128)S(1)}, f32[8]{0:T(128)S(1)}) all-reduce(f32[8,128]{1,0:T(8,128)S(1)} %multiply_reduce_fusion, f32[8]{0:T(128)S(1)} %get-tuple-element.9), channel_id=1, replica_groups=mesh['row'=8,'col'=16,'pan'=2] {'row'}, use_global_device_ids=true, to_apply=%region_8.10 | all-reduce | flops 1032 | bytes 8256 | tf_op jit(solution)/shard_map/psum | solution.py:92
  289.5 3.8 multiply_convert_fusion
  293.4 6.3 %convolution_convert_fusion = bf16[32,1024,128]{2,0,1:T(8,128)(2,1)S(1)} fusion(bf16[1024,8,128]{2,0,1:T(8,128)(2,1)S(1)} %multiply_convert_fusion, s32[32]{0:T(128)S(1)} %eq.91), kind=kOutput, calls=%fused_computation.7 | convolution fusion | flops 71303424 | bytes 10485888 | tf_op jit(solution)/shard_map/ik,rkh->irh/dot_general | solution.py:95
  299.7 8.0 %copy.60 = bf16[16,2,1024,128]{3,1,2,0:T(2,128)(2,1)S(1)} copy(bf16[16,2,1024,128]{3,1,0,2:T(2,128)(2,1)S(1)} %bitcast.91) | data formatting | bytes 16777216 | tf_op jit(solution)/shard_map/reshape | solution.py:98
  307.8 99.0 %all_to_all.16 = bf16[16,2,1024,128]{3,1,2,0:T(2,128)(2,1)S(1)} all-to-all(bf16[16,2,1024,128]{3,1,2,0:T(2,128)(2,1)S(1)} %copy.60), channel_id=1, replica_groups=mesh['row'=8,'col'=16,'pan'=2] {'col'}, dimensions={0} | all-to-all | bytes 16777216 | tf_op jit(solution)/shard_map/all_to_all | solution.py:99
  406.8 6.0 %fusion.32 = bf16[1024,8,128]{2,1,0:T(8,128)(2,1)} fusion(bf16[16,2,1024,128]{3,1,2,0:T(2,128)(2,1)S(1)} %all_to_all.16, pred[2,8]{1,0:T(4,128)(4,1)S(1)} %iota_compare_fusion.4, pred[16,8]{0,1:T(8,128)(4,1)S(1)} %iota_compare_fusion.3), kind=kOutput, calls=%fused_computation.36 | convolution fusion | flops 68157696 | bytes 10485904 | tf_op jit(solution)/shard_map/dcs,dcrh->rsh/dot_general | solution.py:100
  (54 shorter events, 11.7 us)
Async XLA Ops:
  7.2 190.1 %copy-start = (bf16[8,6,256,128]{3,2,1,0:T(8,128)(2,1)S(1)}, bf16[8,6,256,128]{3,2,1,0:T(8,128)(2,1)}, u32[]{:S(2)}) copy-start(bf16[8,6,256,128]{3,2,1,0:T(8,128)(2,1)} %param.16) | copy-start | bytes 9437188
  9.8 50.8 %all-to-all-start = ((s32[16,1,2]{2,1,0:T(1,128)}), s32[16,1,2]{2,1,0:T(1,128)S(1)}, u32[]{:S(2)}, u32[]{:S(2)}) async-start(s32[16,1,2]{2,1,0:T(1,128)} %copy.46), calls=%async_computation | async-start | bytes 16384 | tf_op jit(solution)/shard_map/all_to_all | solution.py:73
  33.3 2.8 copy-start.3
  33.3 2.8 copy-start.4
  36.2 1.6 copy-start.2
  60.6 127.3 %all-to-all-start.1 = ((bf16[16,2,1024,128]{3,2,1,0:T(8,128)(2,1)}), bf16[16,2,1024,128]{3,2,1,0:T(8,128)(2,1)}, u32[]{:S(2)}, u32[]{:S(2)}) async-start(bf16[16,2,1024,128]{3,2,1,0:T(8,128)(2,1)} %copy.54), calls=%async_computation.1 | async-start | bytes 16777216 | tf_op jit(solution)/shard_map/all_to_all | solution.py:72
  67.8 151.7 %all-gather.2.cloned.1.call-start = ((), (), s32[]{:S(2)}) async-start(), calls=%async_computation.3 | async-start | bytes 6291456 | tf_op jit(solution)/shard_map/all_gather | solution.py:84
  187.9 9.4 %copy-start.9 = (s32[8,6]{1,0:T(8,128)S(1)}, s32[8,6]{1,0:T(8,128)}, u32[]{:S(2)}) copy-start(s32[8,6]{1,0:T(8,128)} %param.17) | copy-start | bytes 580
  197.2 22.3 %copy-start.7 = (f32[8,128]{1,0:T(8,128)S(1)}, f32[8,128]{1,0:T(8,128)}, u32[]{:S(2)}) copy-start(f32[8,128]{1,0:T(8,128)} %param.21) | copy-start | bytes 12292
  197.3 22.3 %copy-start.8 = (f32[1024]{0:T(1024)S(1)}, f32[1024]{0:T(1024)}, u32[]{:S(2)}) copy-start(f32[1024]{0:T(1024)} %param.20) | copy-start | bytes 12292
  219.5 48.9 %copy-start.10 = (f32[1024]{0:T(1024)S(1)}, f32[1024]{0:T(1024)}, u32[]{:S(2)}) copy-start(f32[1024]{0:T(1024)} %param.18) | copy-start | bytes 12292
  229.6 59.8 %copy-start.11 = (f32[8,128]{1,0:T(8,128)S(1)}, f32[8,128]{1,0:T(8,128)}, u32[]{:S(2)}) copy-start(f32[8,128]{1,0:T(8,128)} %param.19) | copy-start | bytes 12292
  268.5 24.9 %copy-start.5 = (f32[1024]{0:T(1024)}, f32[1024]{0:T(1024)S(1)}, u32[]{:S(2)}) copy-start(f32[1024]{0:T(1024)S(1)} %multiply_divide_fusion) | copy-start | bytes 12292
  289.5 10.2 %copy-start.6 = (f32[8,128]{1,0:T(8,128)}, f32[8,128]{1,0:T(8,128)S(1)}, u32[]{:S(2)}) copy-start(f32[8,128]{1,0:T(8,128)S(1)} %select_divide_fusion) | copy-start | bytes 12292
  307.8 105.0 %copy-start.1 = (bf16[8,6,256,128]{3,2,1,0:T(8,128)(2,1)S(1)}, bf16[8,6,256,128]{3,2,1,0:T(8,128)(2,1)}, u32[]{:S(2)}) copy-start(bf16[8,6,256,128]{3,2,1,0:T(8,128)(2,1)} %param.16) | copy-start | bytes 9437188
Sparse Core Ops, SparseCore 0:
  197.3 22.1 all-gather.1
